TPU v7x, 32 devices: a whole 2x2x4 slice. The times are simulated.
32 devices in a mesh: lat: 8 (over y, x, core), lon: 4 (over z).
Axes of the slice: x: 2, y: 2, z: 4, core: 2. Of those that a mesh axis runs over, the one named last changes fastest.
Arguments:
- tracers: float32 [4, 4, 256, 720], P(None, None, 'lat', 'lon'), may hold values from -6 to 6
- courant: float32 [2, 4, 256, 720], P(None, None, 'lat', 'lon'), may hold values from -0.8 to 0.8
- cutoffs: int32 [256], replicated, may hold values from 1 to 360, as said below
Outputs:
- updated: float32 [4, 4, 256, 720], P(None, None, 'lat', 'lon')
- filtered_zonal: float32 [4, 256, 720], P(None, 'lat', 'lon')
Inputs may be any that keep to these rules, and one draw needn't show every extreme that they name: cutoffs[j] is 360 for every row j with min(j, 255 - j) >= 64, below 360 for all other rows, and 1 at the two pole rows.
All inputs are finite; a program needn't handle non-finite values.
Results may differ from a plain program's by a relative error of at most 0.0003.
Values sent between devices are 32-bit elements; how exact they have to be, the bound alone decides.
A program may use at most 64 MiB of HBM per device.

v0:
```python
import math
import jax
import numpy as np
import jax.numpy as jnp
from jax import lax
from jax.sharding import PartitionSpec as P


def padded(cells, sides, width, closed):
    for axis, dim in sides:
        count = lax.axis_size(axis)
        ends = count if closed else count - 1
        head = lax.slice_in_dim(cells, 0, width, axis=dim)
        tail = lax.slice_in_dim(cells, cells.shape[dim] - width, cells.shape[dim], axis=dim)
        cells = jnp.concatenate(
            [
                lax.ppermute(tail, axis, [(i, (i + 1) % count) for i in range(ends)]),
                cells,
                lax.ppermute(head, axis, [((i + 1) % count, i) for i in range(ends)]),
            ],
            axis=dim,
        )
    return cells


def take_range(values, start, count, axis_index):
    return lax.slice_in_dim(values, start, start + count, axis=axis_index)


def ppm_flux(extended, courant_faces, axis_index):
    cell_count = extended.shape[axis_index] - 6
    edge_values = 7.0 / 12.0 * (
        take_range(extended, 1, cell_count + 3, axis_index)
        + take_range(extended, 2, cell_count + 3, axis_index)
    ) - 1.0 / 12.0 * (
        take_range(extended, 0, cell_count + 3, axis_index)
        + take_range(extended, 3, cell_count + 3, axis_index)
    )
    left_edge = take_range(edge_values, 0, cell_count + 2, axis_index)
    right_edge = take_range(edge_values, 1, cell_count + 2, axis_index)
    centre = take_range(extended, 2, cell_count + 2, axis_index)
    slopes = right_edge - left_edge
    curvature = 6.0 * centre - 3.0 * (left_edge + right_edge)
    upwind = take_range(right_edge, 0, cell_count + 1, axis_index) - 0.5 * courant_faces * (
        take_range(slopes, 0, cell_count + 1, axis_index)
        - (1.0 - courant_faces * (2.0 / 3.0)) * take_range(curvature, 0, cell_count + 1, axis_index)
    )
    downwind = take_range(left_edge, 1, cell_count + 1, axis_index) - 0.5 * courant_faces * (
        take_range(slopes, 1, cell_count + 1, axis_index)
        + (1.0 + courant_faces * (2.0 / 3.0)) * take_range(curvature, 1, cell_count + 1, axis_index)
    )
    return courant_faces * jnp.where(courant_faces > 0, upwind, downwind)


def metric_weights(first_row, row_count, grid_rows):
    faces = first_row + jnp.arange(-1, row_count, dtype=jnp.int32)
    centres = first_row + jnp.arange(row_count, dtype=jnp.int32)
    face_weight = jnp.sin(
        jnp.minimum(faces + 1, grid_rows - 1 - faces).astype(jnp.float32) * (math.pi / grid_rows)
    )
    cell_weight = jnp.sin(
        (jnp.minimum(centres, grid_rows - 1 - centres).astype(jnp.float32) + 0.5)
        * (math.pi / grid_rows)
    )
    return (face_weight, cell_weight)


def angle_table(first_ids, second_ids, period):
    product = first_ids[:, None] * second_ids[None, :] % period
    angles = product.astype(jnp.float32) * (2.0 * math.pi / period)
    return (jnp.cos(angles), jnp.sin(angles))


def spectral_lowpass(row_block, limits, outer_count):
    row_count, circle = row_block.shape
    inner_count = circle // outer_count
    highest = lax.Precision.HIGHEST
    grid_values = row_block.reshape(row_count, outer_count, inner_count)
    outer_ids = jnp.arange(outer_count, dtype=jnp.int32)
    inner_ids = jnp.arange(inner_count, dtype=jnp.int32)
    outer_cos, outer_sin = angle_table(outer_ids, outer_ids, outer_count)
    inner_cos, inner_sin = angle_table(inner_ids, inner_ids, inner_count)
    twiddle_cos, twiddle_sin = angle_table(inner_ids, outer_ids, circle)
    first_real = jnp.einsum("rab,ak->rbk", grid_values, outer_cos, precision=highest)
    first_imag = -jnp.einsum("rab,ak->rbk", grid_values, outer_sin, precision=highest)
    turned_real = first_real * twiddle_cos + first_imag * twiddle_sin
    turned_imag = first_imag * twiddle_cos - first_real * twiddle_sin
    coeff_real = jnp.einsum("rbk,bj->rjk", turned_real, inner_cos, precision=highest) + jnp.einsum(
        "rbk,bj->rjk", turned_imag, inner_sin, precision=highest
    )
    coeff_imag = jnp.einsum("rbk,bj->rjk", turned_imag, inner_cos, precision=highest) - jnp.einsum(
        "rbk,bj->rjk", turned_real, inner_sin, precision=highest
    )
    wavenumber = inner_ids[:, None] * outer_count + outer_ids[None, :]
    folded = jnp.minimum(wavenumber, circle - wavenumber)
    keep_mask = folded[None, :, :] <= limits[:, None, None]
    coeff_real = jnp.where(keep_mask, coeff_real, 0.0)
    coeff_imag = jnp.where(keep_mask, coeff_imag, 0.0)
    back_real = jnp.einsum("rjk,jb->rbk", coeff_real, inner_cos, precision=highest) - jnp.einsum(
        "rjk,jb->rbk", coeff_imag, inner_sin, precision=highest
    )
    back_imag = jnp.einsum("rjk,jb->rbk", coeff_imag, inner_cos, precision=highest) + jnp.einsum(
        "rjk,jb->rbk", coeff_real, inner_sin, precision=highest
    )
    reverted_real = back_real * twiddle_cos - back_imag * twiddle_sin
    reverted_imag = back_imag * twiddle_cos + back_real * twiddle_sin
    signal = jnp.einsum("rbk,ka->rab", reverted_real, outer_cos, precision=highest) - jnp.einsum(
        "rbk,ka->rab", reverted_imag, outer_sin, precision=highest
    )
    return (signal / circle).reshape(row_count, circle)


def dense_tables(circle):
    half = circle // 2
    cell_ids = np.arange(circle, dtype=np.int64)
    cos_ids = np.arange(half + 1, dtype=np.int64)
    sin_ids = np.arange(1, half, dtype=np.int64)
    forward = np.concatenate(
        [
            np.cos(2.0 * np.pi * (cell_ids[:, None] * cos_ids[None, :] % circle) / circle),
            np.sin(2.0 * np.pi * (cell_ids[:, None] * sin_ids[None, :] % circle) / circle),
        ],
        axis=1,
    )
    out_ids = np.arange(-1, circle, dtype=np.int64)
    cos_scale = np.where((cos_ids == 0) | (cos_ids == half), 1.0, 2.0) / circle
    inverse = np.concatenate(
        [
            cos_scale[:, None]
            * np.cos(2.0 * np.pi * (cos_ids[:, None] * out_ids[None, :] % circle) / circle),
            2.0
            / circle
            * np.sin(2.0 * np.pi * (sin_ids[:, None] * out_ids[None, :] % circle) / circle),
        ],
        axis=0,
    )
    wavenumber = np.concatenate([cos_ids, sin_ids]).astype(np.int32)
    return (
        jnp.asarray(forward.astype(np.float32)),
        jnp.asarray(inverse.astype(np.float32)),
        jnp.asarray(wavenumber),
    )


def dense_lowpass(row_block, limits):
    circle = row_block.shape[1]
    forward, inverse, wavenumber = dense_tables(circle)
    highest = lax.Precision.HIGHEST
    coeff = jnp.dot(row_block, forward, precision=highest)
    coeff = jnp.where(wavenumber[None, :] <= limits[:, None], coeff, 0.0)
    return jnp.dot(coeff, inverse, precision=highest)


def circle_filter(row_block, limits, lon_groups):
    row_count, block_cols = row_block.shape
    whole_rows = lax.all_to_all(row_block, "lon", split_axis=0, concat_axis=1, tiled=True)
    circle = whole_rows.shape[1]
    held_count = row_count // lon_groups
    row_limits = lax.dynamic_slice_in_dim(limits, lax.axis_index("lon") * held_count, held_count)
    whole_ext = jnp.concatenate([whole_rows[:, -1:], whole_rows], axis=1)
    if circle <= 2048:
        lowpass_ext = dense_lowpass(whole_rows, row_limits)
    else:
        lowpass = spectral_lowpass(whole_rows, row_limits, lon_groups)
        lowpass_ext = jnp.concatenate([lowpass[:, -1:], lowpass], axis=1)
    lowpass_ext = jnp.where((row_limits < circle // 2)[:, None], lowpass_ext, whole_ext)
    slabs = jnp.stack(
        [lowpass_ext[:, k * block_cols : (k + 1) * block_cols + 1] for k in range(lon_groups)],
        axis=0,
    )
    back = lax.all_to_all(slabs, "lon", split_axis=0, concat_axis=1, tiled=True)
    return back.reshape(row_count, block_cols + 1)


def body(tracers, courant, cutoffs):
    levels, tracer_count, lat_rows, lon_cols = tracers.shape
    lon_groups = lax.axis_size("lon")
    lat_bands = lax.axis_size("lat")
    band_index = lax.axis_index("lat")
    grid_rows = lat_rows * lat_bands
    zonal = courant[0]
    meridional = courant[1]
    lat_stack = jnp.concatenate([tracers, meridional[:, None]], axis=1)
    lat_ext = padded(lat_stack, (("lat", 2),), 3, False)
    lon_ext = padded(tracers, (("lon", 3),), 3, True)
    flat_count = levels * lat_rows
    flat_zonal = zonal.reshape(flat_count, lon_cols)
    local_limits = lax.dynamic_slice_in_dim(cutoffs, band_index * lat_rows, lat_rows)
    filtered_flat = circle_filter(flat_zonal, jnp.tile(local_limits, levels), lon_groups)
    zonal_faces = filtered_flat.reshape(levels, 1, lat_rows, lon_cols + 1)
    filtered_zonal = zonal_faces[:, 0, :, 1:]
    flux_east = ppm_flux(lon_ext, zonal_faces, 3)
    face_weight, cell_weight = metric_weights(band_index * lat_rows, lat_rows, grid_rows)
    flux_north = (
        ppm_flux(lat_ext[:, :tracer_count], lat_ext[:, tracer_count:, 2 : lat_rows + 3, :], 2)
        * face_weight[None, None, :, None]
    )
    change = (
        flux_east[:, :, :, 1:]
        - flux_east[:, :, :, :-1]
        + (flux_north[:, :, 1:, :] - flux_north[:, :, :-1, :]) / cell_weight[None, None, :, None]
    )
    return (tracers - change, filtered_zonal)


def solution(mesh):
    in_specs = (P(None, None, "lat", "lon"), P(None, None, "lat", "lon"), P())
    out_specs = (P(None, None, "lat", "lon"), P(None, "lat", "lon"))
    return jax.shard_map(body, mesh=mesh, in_specs=in_specs, out_specs=out_specs, check_vma=False)
```

profile of v0, /device:TPU:0, one launch (start us, length us, event | category | flops | bytes accessed | tf_op | source)
XLA Modules:
  0.0 59.9 jit_solution(7719575748991586604)
XLA Ops:
  0.6 0.0 copy-start
  0.6 0.0 copy-start.10
  0.7 1.7 %slice_bitcast_fusion.2 = (f32[4,32,180]{2,1,0:T(8,128)}, f32[4,1,32,180]{3,2,1,0:T(8,128)S(1)}) fusion(f32[2,4,32,180]{3,2,1,0:T(8,128)} %param.7), kind=kLoop, calls=%fused_computation.59 | loop fusion | bytes 368640 | tf_op jit(solution)/shard_map/all_to_all | solution.py:156
  2.4 0.0 copy-start.2
  2.4 1.1 %pad_maximum_fusion.9 = (f32[4,5,3,180]{3,2,1,0:T(4,128)S(1)}, f32[4,5,3,180]{3,2,1,0:T(4,128)S(1)}) fusion(f32[4,1,32,180]{3,2,1,0:T(8,128)S(1)} %get-tuple-element.15, f32[4,4,32,180]{3,2,1,0:T(8,128)} %param.6), kind=kLoop, calls=%fused_computation.63 | loop fusion | flops 21600 | bytes 547200 | tf_op jit(solution)/shard_map/slice | solution.py:14
  3.4 1.3 %collective-permute-start.3 = (f32[4,5,3,180]{3,2,1,0:T(4,128)S(1)}, f32[4,5,3,180]{3,2,1,0:T(4,128)S(1)}, u32[]{:S(2)}, u32[]{:S(2)}) collective-permute-start(f32[4,5,3,180]{3,2,1,0:T(4,128)S(1)} %get-tuple-element.9), channel_id=1, source_target_pairs={{4,0},{8,4},{12,8},{16,12},{20,16},{24,20},{28,24},{5,1},{9,5},{13... | collective-permute-start | bytes 129608 | tf_op jit(solution)/shard_map/ppermute | solution.py:19
  4.7 3.0 %collective-permute-start.2 = (f32[4,5,3,180]{3,2,1,0:T(4,128)S(1)}, f32[4,5,3,180]{3,2,1,0:T(4,128)S(1)}, u32[]{:S(2)}, u32[]{:S(2)}) collective-permute-start(f32[4,5,3,180]{3,2,1,0:T(4,128)S(1)} %get-tuple-element.8), channel_id=1, source_target_pairs={{0,4},{4,8},{8,12},{12,16},{16,20},{20,24},{24,28},{1,5},{5,9},{9,... | collective-permute-start | bytes 129608 | tf_op jit(solution)/shard_map/ppermute | solution.py:17
  7.8 1.2 %fusion.34 = (f32[4,4,32,3]{3,2,1,0:T(8,128)S(1)}, f32[4,4,32,3]{3,2,1,0:T(8,128)S(1)}) fusion(f32[4,4,32,180]{3,2,1,0:T(8,128)} %param.6), kind=kLoop, calls=%fused_computation.77 | loop fusion | bytes 24576 | tf_op jit(solution)/shard_map/slice | solution.py:14
  8.9 5.1 %collective-permute-start.1 = (f32[4,4,32,3]{3,2,1,0:T(8,128)S(1)}, f32[4,4,32,3]{3,2,1,0:T(8,128)S(1)}, u32[]{:S(2)}, u32[]{:S(2)}) collective-permute-start(f32[4,4,32,3]{3,2,1,0:T(8,128)S(1)} %get-tuple-element.13), channel_id=1, source_target_pairs={{1,0},{2,1},{3,2},{0,3},{5,4},{6,5},{7,6},{4,7},{9,8},{10,9},{11,1... | collective-permute-start | bytes 18440 | tf_op jit(solution)/shard_map/ppermute | solution.py:19
  14.1 0.0 collective-permute-start
  14.1 5.1 %all-to-all-start = ((f32[4,32,180]{2,1,0:T(8,128)}), f32[4,32,180]{2,1,0:T(8,128)}, u32[]{:S(2)}, u32[]{:S(2)}) async-start(f32[4,32,180]{2,1,0:T(8,128)} %get-tuple-element.14), calls=%async_computation | async-start | bytes 262144 | tf_op jit(solution)/shard_map/all_to_all | solution.py:156
  19.2 0.0 copy-done.10
  19.2 0.1 dynamic_slice.6
  19.3 0.1 tile.10
  19.4 0.1 broadcast_compare_fusion.1
  19.5 0.6 fusion.33
  20.0 0.6 %collective-permute-done.1 = f32[4,4,32,3]{3,2,1,0:T(8,128)S(1)} collective-permute-done((f32[4,4,32,3]{3,2,1,0:T(8,128)S(1)}, f32[4,4,32,3]{3,2,1,0:T(8,128)S(1)}, u32[]{:S(2)}, u32[]{:S(2)}) %collective-permute-start.1) | collective-permute-done | bytes 6176 | tf_op jit(solution)/shard_map/ppermute | solution.py:19
  20.7 6.6 %collective-permute-done = f32[4,4,32,3]{3,2,1,0:T(8,128)S(1)} collective-permute-done((f32[4,4,32,3]{3,2,1,0:T(8,128)S(1)}, f32[4,4,32,3]{3,2,1,0:T(8,128)S(1)}, u32[]{:S(2)}, u32[]{:S(2)}) %collective-permute-start) | collective-permute-done | bytes 6176 | tf_op jit(solution)/shard_map/ppermute | solution.py:17
  27.2 0.0 copy-done
  27.2 0.3 pad_maximum_fusion.5
  27.5 0.6 fusion.28
  28.1 1.1 %slice_subtract_fusion.3 = (f32[4,4,32,182]{3,2,1,0:T(8,128)S(1)}, f32[4,4,32,182]{3,2,1,0:T(8,128)}) fusion(f32[4,4,32,183]{3,2,1,0:T(8,128)S(1)} %fusion.28, f32[4,4,32,186]{3,2,1,0:T(8,128)S(1)} %pad_maximum_fusion.5), kind=kLoop, calls=%fused_computation.50 | loop fusion | flops 465920 | bytes 1863680 | tf_op jit(solution)/shard_map/sub | solution.py:42
  29.2 0.0 collective-permute-done.3
  29.2 0.0 collective-permute-done.2
  29.2 0.0 copy-start.6
  29.2 0.1 pad_maximum_fusion
  29.3 0.0 copy-done.2
  29.4 0.5 copy-done.6
  29.8 0.3 fusion.13
  30.1 0.0 copy-start.3
  30.1 0.0 copy-start.7
  30.1 0.0 copy-start.8
  30.2 0.2 slice_subtract_fusion
  30.4 0.7 %copy-done.3 = f32[4,1,32,180]{3,2,1,0:T(8,128)S(1)} copy-done((f32[4,1,32,180]{3,2,1,0:T(8,128)S(1)}, f32[4,1,32,180]{3,2,1,0:T(8,128)}, u32[]{:S(2)}) %copy-start.3) | copy-done | bytes 92184
  31.0 0.0 copy-done.7
  31.1 0.7 %compare_bitcast_fusion = (pred[4,33,180]{2,1,0:T(8,128)(4,1)}, f32[4,1,33,180]{3,2,1,0:T(8,128)}) fusion(f32[4,1,32,180]{3,2,1,0:T(8,128)S(1)} %copy-done.3, f32[4,4,32,180]{3,2,1,0:T(8,128)S(1)} %copy-done, f32[4,5,3,180]{3,2,1,0:T(4,128)S(1)} %copy-done.7), kind=kLoop, calls=%fused_computation.55 | loop fusion | flops 71280 | bytes 622800 | tf_op jit(solution)/shard_map/jit(_where)/broadcast_in_dim | solution.py:52
  31.8 1.7 %multiply_bitcast_fusion = (f32[4,33,180]{2,1,0:T(8,128)}, f32[4,33,180]{2,1,0:T(8,128)}, f32[4,33,180]{2,1,0:T(8,128)}) fusion(f32[4,1,33,180]{3,2,1,0:T(8,128)} %get-tuple-element.5), kind=kLoop, calls=%fused_computation.54 | loop fusion | flops 95040 | bytes 380160 | tf_op jit(solution)/shard_map/mul | solution.py:44
  33.5 0.0 all-to-all-done
  33.5 1.6 %copy.8 = f32[32,4,180]{2,1,0:T(4,128)} copy(f32[32,4,180]{2,0,1:T(8,128)} %bitcast.1) | data formatting | bytes 184320 | tf_op jit(solution)/shard_map/all_to_all | solution.py:156
  35.2 1.7 %all_to_all.26 = f32[32,720]{1,0:T(8,128)} reshape(f32[32,4,180]{2,1,0:T(4,128)} %copy.8) | data formatting | bytes 184320 | tf_op jit(solution)/shard_map/all_to_all | solution.py:156
  36.9 0.0 copy-start.4
  36.9 0.0 copy-start.5
  36.9 0.9 %slice.175 = f32[32,1]{1,0:T(8,128)S(1)} slice(f32[32,720]{1,0:T(8,128)} %all_to_all.26), slice={[0:32], [719:720]} | slice | bytes 256 | tf_op jit(solution)/shard_map/slice | solution.py:160
  37.8 0.0 copy-done.8
  37.8 3.0 %fusion = f32[32,720]{1,0:T(8,128)S(1)} fusion(f32[720,720]{1,0:T(8,128)} %constant.14.clone, f32[32,720]{1,0:T(8,128)} %all_to_all.26, s32[720]{0:T(1024)S(1)} %copy-done.8, s32[32]{0:T(128)S(1)} %get-tuple-element.3), kind=kOutput, calls=%fused_computation.2 | convolution fusion | flops 199111680 | bytes 2260928 | tf_op jit(solution)/shard_map/dot_general | solution.py:149
  40.8 0.0 copy-done.4
  40.8 0.0 copy-done.5
  40.8 1.4 %convolution_select_fusion = f32[32,721]{1,0:T(8,128)S(1)} fusion(f32[32,720]{1,0:T(8,128)S(1)} %fusion, f32[720,721]{1,0:T(8,128)S(1)} %copy-done.4, f32[32,720]{1,0:T(8,128)S(1)} %copy-done.5, f32[32,1]{1,0:T(8,128)S(1)} %slice.175, pred[32]{0:T(512)(128)(4,1)S(1)} %get-tuple-element.2), kind=kOutput, calls=%fused_computation | convolution fusion | flops 199388224 | bytes 2353248 | tf_op jit(solution)/shard_map/dot_general | solution.py:151
  42.2 0.1 slice_bitcast_fusion.6
  42.3 0.7 %pad_maximum_fusion.7 = f32[4,32,181]{2,1,0:T(8,128)} fusion(f32[1,32,181]{2,1,0:T(8,128)S(1)} %get-tuple-element.23, f32[1,32,181]{2,1,0:T(8,128)S(1)} %get-tuple-element.24, f32[1,32,181]{2,1,0:T(8,128)S(1)} %get-tuple-element.25, f32[1,32,181]{2,1,0:T(8,128)S(1)} %get-tuple-element.22), kind=kLoop, calls=%fused_computation.57 | loop fusion | flops 69504 | bytes 185344 | tf_op jit(solution)/shard_map/stack | solution.py:167
  42.9 4.0 %all-to-all-start.1 = ((f32[4,32,181]{2,1,0:T(8,128)}), f32[4,32,181]{2,1,0:T(8,128)}, u32[]{:S(2)}, u32[]{:S(2)}) async-start(f32[4,32,181]{2,1,0:T(8,128)} %pad_maximum_fusion.7), calls=%async_computation.1 | async-start | bytes 262144 | tf_op jit(solution)/shard_map/all_to_all | solution.py:171
  46.9 2.4 %fusion.6 = f32[4,4,33,180]{3,2,1,0:T(8,128)} fusion(f32[4,4,34,180]{3,2,1,0:T(8,128)S(1)} %get-tuple-element.7, f32[4,4,34,180]{3,2,1,0:T(8,128)S(1)} %get-tuple-element.6, f32[4,4,35,180]{3,2,1,0:T(8,128)S(1)} %fusion.13, f32[33]{0:T(128)S(1)} %multiply_sine_fusion, f32[4,33,180]{2,1,0:T(8,128)} %get-tuple-element.18, f32[4,33,180]{2,1,0:T(8,128)} %get-tuple-element.17, ...), kind=kLoop, calls=%fused_computation.10 | loop fusion | flops 1045440 | bytes 2685012 | tf_op jit(solution)/shard_map/mul | solution.py:195
  49.3 4.2 %all-to-all-done.1 = f32[4,32,181]{2,1,0:T(8,128)} async-done(((f32[4,32,181]{2,1,0:T(8,128)}), f32[4,32,181]{2,1,0:T(8,128)}, u32[]{:S(2)}, u32[]{:S(2)}) %all-to-all-start.1) | async-done | bytes 92704 | tf_op jit(solution)/shard_map/all_to_all | solution.py:171
  53.5 1.7 %slice_bitcast_fusion = f32[4,32,180]{2,1,0:T(8,128)} fusion(f32[4,1,32,181]{3,2,0,1:T(8,128)} %bitcast.13), kind=kLoop, calls=%fused_computation.56 | loop fusion | bytes 184320 | tf_op jit(solution)/shard_map/squeeze | solution.py:191
  55.2 0.0 copy-start.1
  55.2 0.0 copy-start.9
  55.2 1.0 %broadcast_multiply_fusion = (f32[4,32,181]{2,1,0:T(8,128)S(1)}, f32[4,32,181]{2,1,0:T(8,128)S(1)}, f32[4,32,181]{2,1,0:T(8,128)S(1)}) fusion(f32[4,32,181]{2,1,0:T(8,128)} %all-to-all-done.1), kind=kLoop, calls=%fused_computation.64 | loop fusion | flops 92672 | bytes 370688 | tf_op jit(solution)/shard_map/mul | solution.py:44
  56.2 0.9 %broadcast_compare_fusion = pred[4,32,181]{2,1,0:T(8,128)(4,1)S(1)} fusion(f32[4,32,181]{2,1,0:T(8,128)} %all-to-all-done.1), kind=kLoop, calls=%fused_computation.65 | loop fusion | flops 23168 | bytes 115840 | tf_op jit(solution)/shard_map/gt | solution.py:52
  57.1 1.8 %fusion.22 = f32[4,4,32,181]{3,2,1,0:T(8,128)S(1)} fusion(f32[4,4,32,182]{3,2,1,0:T(8,128)} %get-tuple-element.11, f32[4,4,32,182]{3,2,1,0:T(8,128)S(1)} %get-tuple-element.10, f32[4,4,32,183]{3,2,1,0:T(8,128)S(1)} %fusion.28, f32[4,32,181]{2,1,0:T(8,128)S(1)} %get-tuple-element.20, f32[4,32,181]{2,1,0:T(8,128)S(1)} %get-tuple-element.21, ...), kind=kLoop, calls=%fused_computation.37 | loop fusion | flops 926720 | bytes 2617984 | tf_op jit(solution)/shard_map/mul | solution.py:52
  58.9 0.0 copy-done.1
  58.9 0.0 copy-done.9
  58.9 1.0 %fusion.17 = f32[4,4,32,180]{3,2,1,0:T(8,128)} fusion(f32[4,4,32,180]{3,2,1,0:T(8,128)S(1)} %copy-done, f32[4,4,33,180]{3,2,1,0:T(8,128)S(1)} %copy-done.1, f32[4,4,32,181]{3,2,1,0:T(8,128)S(1)} %fusion.22, f32[32]{0:T(128)S(1)} %copy-done.9), kind=kLoop, calls=%fused_computation.30 | loop fusion | flops 460800 | bytes 2211968 | tf_op jit(solution)/shard_map/sub | solution.py:203
  (2 shorter events, 0.1 us)
Async XLA Ops:
  0.6 26.6 %copy-start = (f32[4,4,32,180]{3,2,1,0:T(8,128)S(1)}, f32[4,4,32,180]{3,2,1,0:T(8,128)}, u32[]{:S(2)}) copy-start(f32[4,4,32,180]{3,2,1,0:T(8,128)} %param.6) | copy-start | bytes 1105924
  0.6 18.6 %copy-start.10 = (s32[256]{0:T(256)S(1)}, s32[256]{0:T(256)}, u32[]{:S(2)}) copy-start(s32[256]{0:T(256)} %param.8) | copy-start | bytes 3076
  2.4 27.0 %copy-start.2 = (f32[4,1,32,180]{3,2,1,0:T(8,128)}, f32[4,1,32,180]{3,2,1,0:T(8,128)S(1)}, u32[]{:S(2)}) copy-start(f32[4,1,32,180]{3,2,1,0:T(8,128)S(1)} %get-tuple-element.15) | copy-start | bytes 276484
  3.4 25.8 %collective-permute-start.3 = (f32[4,5,3,180]{3,2,1,0:T(4,128)S(1)}, f32[4,5,3,180]{3,2,1,0:T(4,128)S(1)}, u32[]{:S(2)}, u32[]{:S(2)}) collective-permute-start(f32[4,5,3,180]{3,2,1,0:T(4,128)S(1)} %get-tuple-element.9), channel_id=1, source_target_pairs={{4,0},{8,4},{12,8},{16,12},{20,16},{24,20},{28,24},{5,1},{9,5},{13... | collective-permute-start | bytes 129608 | tf_op jit(solution)/shard_map/ppermute | solution.py:19
  4.7 24.5 %collective-permute-start.2 = (f32[4,5,3,180]{3,2,1,0:T(4,128)S(1)}, f32[4,5,3,180]{3,2,1,0:T(4,128)S(1)}, u32[]{:S(2)}, u32[]{:S(2)}) collective-permute-start(f32[4,5,3,180]{3,2,1,0:T(4,128)S(1)} %get-tuple-element.8), channel_id=1, source_target_pairs={{0,4},{4,8},{8,12},{12,16},{16,20},{20,24},{24,28},{1,5},{5,9},{9,... | collective-permute-start | bytes 129608 | tf_op jit(solution)/shard_map/ppermute | solution.py:17
  8.9 11.7 %collective-permute-start.1 = (f32[4,4,32,3]{3,2,1,0:T(8,128)S(1)}, f32[4,4,32,3]{3,2,1,0:T(8,128)S(1)}, u32[]{:S(2)}, u32[]{:S(2)}) collective-permute-start(f32[4,4,32,3]{3,2,1,0:T(8,128)S(1)} %get-tuple-element.13), channel_id=1, source_target_pairs={{1,0},{2,1},{3,2},{0,3},{5,4},{6,5},{7,6},{4,7},{9,8},{10,9},{11,1... | collective-permute-start | bytes 18440 | tf_op jit(solution)/shard_map/ppermute | solution.py:19
  14.1 13.2 %collective-permute-start = (f32[4,4,32,3]{3,2,1,0:T(8,128)S(1)}, f32[4,4,32,3]{3,2,1,0:T(8,128)S(1)}, u32[]{:S(2)}, u32[]{:S(2)}) collective-permute-start(f32[4,4,32,3]{3,2,1,0:T(8,128)S(1)} %get-tuple-element.12), channel_id=1, source_target_pairs={{0,1},{1,2},{2,3},{3,0},{4,5},{5,6},{6,7},{7,4},{8,9},{9,10},{10,1... | collective-permute-start | bytes 18440 | tf_op jit(solution)/shard_map/ppermute | solution.py:17
  14.1 19.5 %all-to-all-start = ((f32[4,32,180]{2,1,0:T(8,128)}), f32[4,32,180]{2,1,0:T(8,128)}, u32[]{:S(2)}, u32[]{:S(2)}) async-start(f32[4,32,180]{2,1,0:T(8,128)} %get-tuple-element.14), calls=%async_computation | async-start | bytes 262144 | tf_op jit(solution)/shard_map/all_to_all | solution.py:156
  29.2 0.6 %copy-start.6 = (f32[4,5,3,180]{3,2,1,0:T(4,128)}, f32[4,5,3,180]{3,2,1,0:T(4,128)S(1)}, u32[]{:S(2)}) copy-start(f32[4,5,3,180]{3,2,1,0:T(4,128)S(1)} %collective-permute-done.2) | copy-start | bytes 129604
  30.1 0.9 %copy-start.3 = (f32[4,1,32,180]{3,2,1,0:T(8,128)S(1)}, f32[4,1,32,180]{3,2,1,0:T(8,128)}, u32[]{:S(2)}) copy-start(f32[4,1,32,180]{3,2,1,0:T(8,128)} %copy-done.2) | copy-start | bytes 276484
  30.1 0.9 %copy-start.7 = (f32[4,5,3,180]{3,2,1,0:T(4,128)S(1)}, f32[4,5,3,180]{3,2,1,0:T(4,128)}, u32[]{:S(2)}) copy-start(f32[4,5,3,180]{3,2,1,0:T(4,128)} %copy-done.6) | copy-start | bytes 129604
  30.1 7.7 %copy-start.8 = (s32[720]{0:T(1024)S(1)}, s32[720]{0:T(1024)}, u32[]{:S(2)}) copy-start(s32[720]{0:T(1024)} %constant.16.clone) | copy-start | bytes 8644
  36.9 3.9 %copy-start.4 = (f32[720,721]{1,0:T(8,128)S(1)}, f32[720,721]{1,0:T(8,128)}, u32[]{:S(2)}) copy-start(f32[720,721]{1,0:T(8,128)} %constant.15.clone) | copy-start | bytes 6229444
  36.9 3.9 %copy-start.5 = (f32[32,720]{1,0:T(8,128)S(1)}, f32[32,720]{1,0:T(8,128)}, u32[]{:S(2)}) copy-start(f32[32,720]{1,0:T(8,128)} %all_to_all.26) | copy-start | bytes 276484
  42.9 10.6 %all-to-all-start.1 = ((f32[4,32,181]{2,1,0:T(8,128)}), f32[4,32,181]{2,1,0:T(8,128)}, u32[]{:S(2)}, u32[]{:S(2)}) async-start(f32[4,32,181]{2,1,0:T(8,128)} %pad_maximum_fusion.7), calls=%async_computation.1 | async-start | bytes 262144 | tf_op jit(solution)/shard_map/all_to_all | solution.py:171
  55.2 3.7 %copy-start.1 = (f32[4,4,33,180]{3,2,1,0:T(8,128)S(1)}, f32[4,4,33,180]{3,2,1,0:T(8,128)}, u32[]{:S(2)}) copy-start(f32[4,4,33,180]{3,2,1,0:T(8,128)} %fusion.6) | copy-start | bytes 1140484
  55.2 3.7 %copy-start.9 = (f32[32]{0:T(128)S(1)}, f32[32]{0:T(128)}, u32[]{:S(2)}) copy-start(f32[32]{0:T(128)} %fusion.33) | copy-start | bytes 388
where the time goes:
time: 60.6 us; the launch traced here: 59.9 us
  starting transfers between devices  18.5 us (31%)
  other arithmetic  14.5 us (24%)
  waiting for transfers between devices  11.4 us (19%)
  local copies, waits for them, and re-layouts  10.3 us (17%)
  matrix products  4.33 us (7%)
  between operations  0.84 us (1%)
    ppermute x2, waiting for transfers between devices, padded(): lax.ppermute(tail, axis, [(i, (i + 1) % count) for i in range(ends)])  6.58 us
    ppermute x2, starting transfers between devices, padded(): lax.ppermute(head, axis, [((i + 1) % count, i) for i in range(ends)])  6.42 us
    all_to_all x1, starting transfers between devices, circle_filter(): lax.all_to_all(row_block, 'lon', split_axis=0, concat_axis=1, tiled=True)  5.09 us
    all_to_all x3, local copies, waits for them, and re-layouts, circle_filter(): lax.all_to_all(row_block, 'lon', split_axis=0, concat_axis=1, tiled=True)  5.04 us
    all_to_all x1, waiting for transfers between devices, circle_filter(): back = lax.all_to_all(slabs, 'lon', split_axis=0, concat_axis=1, tiled=True)  4.23 us
    all_to_all x1, starting transfers between devices, circle_filter(): back = lax.all_to_all(slabs, 'lon', split_axis=0, concat_axis=1, tiled=True)  3.95 us
    ppermute x2, starting transfers between devices, padded(): lax.ppermute(tail, axis, [(i, (i + 1) % count) for i in range(ends)])  3.04 us
    dot_general x1, matrix products, dense_lowpass(): coeff = jnp.dot(row_block, forward, precision=highest)  2.97 us
  transfers between devices with their start and end apart: 6, of which 3 were waited for; matrix products, arithmetic and copies ran while one was open for 16% of the time, Pallas kernels for 0%

commit v1 on v0

--- a/solution.py
+++ b/solution.py
@@ -168,7 +168,19 @@
         [lowpass_ext[:, k * block_cols : (k + 1) * block_cols + 1] for k in range(lon_groups)],
         axis=0,
     )
-    back = lax.all_to_all(slabs, "lon", split_axis=0, concat_axis=1, tiled=True)
+    ways, here = (lax.axis_size("lon"), lax.axis_index("lon"))
+    width_2 = slabs.shape[0] // ways
+    lengths = list(slabs.shape)
+    lengths[0] = width_2
+    height = lengths[1]
+    lengths[1] = height * ways
+    full = jnp.zeros(lengths, slabs.dtype)
+    for mask in range(ways):
+        part = lax.dynamic_slice_in_dim(slabs, (here ^ mask) * width_2, width_2, axis=0)
+        if mask:
+            part = lax.ppermute(part, "lon", [(d, d ^ mask) for d in range(ways)])
+        full = lax.dynamic_update_slice_in_dim(full, part, (here ^ mask) * height, axis=1)
+    back = full
     return back.reshape(row_count, block_cols + 1)
 
 

time: 60.6 us -> 53.7 us (0.89)
  other arithmetic: 14.5 us -> 7.76 us
    ppermute x0 -> x3, starting transfers between devices: none -> 4.52 us  [circle_filter(): part = lax.ppermute(part, 'lon', [(d, d ^ mask) for d in range(ways)])]
    all_to_all x1 -> x0, waiting for transfers between devices: 4.23 us -> none  [circle_filter(): back = lax.all_to_all(slabs, 'lon', split_axis=0, concat_axis=1, tiled=True)]
    all_to_all x1 -> x0, starting transfers between devices: 3.95 us -> none  [circle_filter(): back = lax.all_to_all(slabs, 'lon', split_axis=0, concat_axis=1, tiled=True)]
    ppermute x0 -> x3, waiting for transfers between devices: none -> 3.95 us  [circle_filter(): part = lax.ppermute(part, 'lon', [(d, d ^ mask) for d in range(ways)])]
    mul x1, other arithmetic: 2.4 us -> 0.42 us  [body(): ppm_flux(lat_ext[:, :tracer_count], lat_ext[:, tracer_count:, 2:lat_rows...]
    mul x2, other arithmetic: 2.74 us -> 0.83 us  [ppm_flux(): 0.5 * courant_faces]
    mul x1, other arithmetic: 1.76 us -> 0.5 us  [ppm_flux(): return courant_faces * jnp.where(courant_faces > 0, upwind, downwind)]
    gt x1, other arithmetic: 0.93 us -> 0.02 us  [ppm_flux(): return courant_faces * jnp.where(courant_faces > 0, upwind, downwind)]
  transfers between devices with their start and end apart: 6 -> 8, of which waited for: 3 -> 4; matrix products, arithmetic and copies ran while one was open for 16% -> 12% of each run, Pallas kernels for 0% -> 0%
where the time goes in v1:
time: 53.7 us; the launch traced here: 53.3 us
  starting transfers between devices  19.1 us (36%)
  waiting for transfers between devices  11.1 us (21%)
  local copies, waits for them, and re-layouts  10.1 us (19%)
  other arithmetic  7.76 us (14%)
  matrix products  4.33 us (8%)
  between operations  0.92 us (2%)
    ppermute x2, waiting for transfers between devices, padded(): lax.ppermute(tail, axis, [(i, (i + 1) % count) for i in range(ends)])  6.58 us
    ppermute x2, starting transfers between devices, padded(): lax.ppermute(head, axis, [((i + 1) % count, i) for i in range(ends)])  6.42 us
    all_to_all x1, starting transfers between devices, circle_filter(): lax.all_to_all(row_block, 'lon', split_axis=0, concat_axis=1, tiled=True)  5.09 us
    all_to_all x3, local copies, waits for them, and re-layouts, circle_filter(): lax.all_to_all(row_block, 'lon', split_axis=0, concat_axis=1, tiled=True)  5.02 us
    ppermute x3, starting transfers between devices, circle_filter(): part = lax.ppermute(part, 'lon', [(d, d ^ mask) for d in range(ways)])  4.52 us
    ppermute x3, waiting for transfers between devices, circle_filter(): part = lax.ppermute(part, 'lon', [(d, d ^ mask) for d in range(ways)])  3.95 us
    ppermute x2, starting transfers between devices, padded(): lax.ppermute(tail, axis, [(i, (i + 1) % count) for i in range(ends)])  3.04 us
    dot_general x1, matrix products, dense_lowpass(): coeff = jnp.dot(row_block, forward, precision=highest)  2.97 us
  transfers between devices with their start and end apart: 8, of which 4 were waited for; matrix products, arithmetic and copies ran while one was open for 12% of the time, Pallas kernels for 0%

profile of v1, /device:TPU:0, one launch (start us, length us, event | category | flops | bytes accessed | tf_op | source)
XLA Modules:
  0.0 53.3 jit_solution(266942657313929172)
XLA Ops:
  0.6 0.0 copy-start
  0.6 0.0 copy-start.16
  0.7 1.7 %slice_bitcast_fusion.2 = (f32[4,32,180]{2,1,0:T(8,128)}, f32[4,1,32,180]{3,2,1,0:T(8,128)S(1)}) fusion(f32[2,4,32,180]{3,2,1,0:T(8,128)} %param.7), kind=kLoop, calls=%fused_computation.59 | loop fusion | bytes 368640 | tf_op jit(solution)/shard_map/all_to_all | solution.py:156
  2.4 1.1 %pad_maximum_fusion.9 = (f32[4,5,3,180]{3,2,1,0:T(4,128)S(1)}, f32[4,5,3,180]{3,2,1,0:T(4,128)S(1)}) fusion(f32[4,1,32,180]{3,2,1,0:T(8,128)S(1)} %get-tuple-element.15, f32[4,4,32,180]{3,2,1,0:T(8,128)} %param.6), kind=kLoop, calls=%fused_computation.63 | loop fusion | flops 21600 | bytes 547200 | tf_op jit(solution)/shard_map/slice | solution.py:14
  3.4 1.3 %collective-permute-start.6 = (f32[4,5,3,180]{3,2,1,0:T(4,128)S(1)}, f32[4,5,3,180]{3,2,1,0:T(4,128)S(1)}, u32[]{:S(2)}, u32[]{:S(2)}) collective-permute-start(f32[4,5,3,180]{3,2,1,0:T(4,128)S(1)} %get-tuple-element.9), channel_id=1, source_target_pairs={{4,0},{8,4},{12,8},{16,12},{20,16},{24,20},{28,24},{5,1},{9,5},{13... | collective-permute-start | bytes 129608 | tf_op jit(solution)/shard_map/ppermute | solution.py:19
  4.7 3.0 %collective-permute-start.5 = (f32[4,5,3,180]{3,2,1,0:T(4,128)S(1)}, f32[4,5,3,180]{3,2,1,0:T(4,128)S(1)}, u32[]{:S(2)}, u32[]{:S(2)}) collective-permute-start(f32[4,5,3,180]{3,2,1,0:T(4,128)S(1)} %get-tuple-element.8), channel_id=1, source_target_pairs={{0,4},{4,8},{8,12},{12,16},{16,20},{20,24},{24,28},{1,5},{5,9},{9,... | collective-permute-start | bytes 129608 | tf_op jit(solution)/shard_map/ppermute | solution.py:17
  7.8 1.2 %fusion.34 = (f32[4,4,32,3]{3,2,1,0:T(8,128)S(1)}, f32[4,4,32,3]{3,2,1,0:T(8,128)S(1)}) fusion(f32[4,4,32,180]{3,2,1,0:T(8,128)} %param.6), kind=kLoop, calls=%fused_computation.84 | loop fusion | bytes 24576 | tf_op jit(solution)/shard_map/slice | solution.py:14
  8.9 5.1 %collective-permute-start.4 = (f32[4,4,32,3]{3,2,1,0:T(8,128)S(1)}, f32[4,4,32,3]{3,2,1,0:T(8,128)S(1)}, u32[]{:S(2)}, u32[]{:S(2)}) collective-permute-start(f32[4,4,32,3]{3,2,1,0:T(8,128)S(1)} %get-tuple-element.13), channel_id=1, source_target_pairs={{1,0},{2,1},{3,2},{0,3},{5,4},{6,5},{7,6},{4,7},{9,8},{10,9},{11,1... | collective-permute-start | bytes 18440 | tf_op jit(solution)/shard_map/ppermute | solution.py:19
  14.1 0.0 collective-permute-start.3
  14.1 5.1 %all-to-all-start = ((f32[4,32,180]{2,1,0:T(8,128)}), f32[4,32,180]{2,1,0:T(8,128)}, u32[]{:S(2)}, u32[]{:S(2)}) async-start(f32[4,32,180]{2,1,0:T(8,128)} %get-tuple-element.14), calls=%async_computation | async-start | bytes 262144 | tf_op jit(solution)/shard_map/all_to_all | solution.py:156
  19.2 0.0 copy-done.16
  19.2 0.1 dynamic_slice.18
  19.3 0.1 tile.10
  19.4 0.1 broadcast_compare_fusion.1
  19.5 0.6 %fusion.33 = f32[32]{0:T(128)} fusion(s32[]{:T(128)S(6)} %mul.208), kind=kLoop, calls=%fused_computation.81 | loop fusion | flops 192 | bytes 132 | tf_op jit(solution)/shard_map/sin | solution.py:61
  20.0 0.6 %collective-permute-done.4 = f32[4,4,32,3]{3,2,1,0:T(8,128)S(1)} collective-permute-done((f32[4,4,32,3]{3,2,1,0:T(8,128)S(1)}, f32[4,4,32,3]{3,2,1,0:T(8,128)S(1)}, u32[]{:S(2)}, u32[]{:S(2)}) %collective-permute-start.4) | collective-permute-done | bytes 6176 | tf_op jit(solution)/shard_map/ppermute | solution.py:19
  20.7 6.6 %collective-permute-done.3 = f32[4,4,32,3]{3,2,1,0:T(8,128)S(1)} collective-permute-done((f32[4,4,32,3]{3,2,1,0:T(8,128)S(1)}, f32[4,4,32,3]{3,2,1,0:T(8,128)S(1)}, u32[]{:S(2)}, u32[]{:S(2)}) %collective-permute-start.3) | collective-permute-done | bytes 6176 | tf_op jit(solution)/shard_map/ppermute | solution.py:17
  27.2 0.0 copy-done
  27.2 0.3 pad_maximum_fusion.5
  27.5 0.5 %fusion.28 = f32[4,4,32,183]{3,2,1,0:T(8,128)S(1)} fusion(f32[4,4,32,186]{3,2,1,0:T(8,128)S(1)} %pad_maximum_fusion.5, f32[4,4,32,180]{3,2,1,0:T(8,128)S(1)} %copy-done, f32[4,4,32,3]{3,2,1,0:T(8,128)S(1)} %collective-permute-done.3, f32[4,4,32,3]{3,2,1,0:T(8,128)S(1)} %collective-permute-done.4), kind=kLoop, calls=%fused_computation.46 | loop fusion | flops 655872 | bytes 1505280 | tf_op jit(solution)/shard_map/sub | solution.py:32
  28.1 1.1 %slice_subtract_fusion.3 = (f32[4,4,32,182]{3,2,1,0:T(8,128)S(1)}, f32[4,4,32,182]{3,2,1,0:T(8,128)}) fusion(f32[4,4,32,183]{3,2,1,0:T(8,128)S(1)} %fusion.28, f32[4,4,32,186]{3,2,1,0:T(8,128)S(1)} %pad_maximum_fusion.5), kind=kLoop, calls=%fused_computation.50 | loop fusion | flops 465920 | bytes 1863680 | tf_op jit(solution)/shard_map/sub | solution.py:42
  29.2 0.0 collective-permute-done.6
  29.2 0.0 collective-permute-done.5
  29.2 0.1 pad_maximum_fusion
  29.3 0.0 copy-done.2
  29.3 0.5 copy-done.8
  29.8 0.3 fusion.13
  30.1 0.0 copy-start.3
  30.1 0.0 copy-start.9
  30.1 0.0 copy-start.14
  30.1 0.2 slice_subtract_fusion
  30.3 0.7 %copy-done.3 = f32[4,1,32,180]{3,2,1,0:T(8,128)S(1)} copy-done((f32[4,1,32,180]{3,2,1,0:T(8,128)S(1)}, f32[4,1,32,180]{3,2,1,0:T(8,128)}, u32[]{:S(2)}) %copy-start.3) | copy-done | bytes 92184
  31.0 0.0 copy-done.9
  31.0 0.7 %compare_bitcast_fusion = (pred[4,33,180]{2,1,0:T(8,128)(4,1)}, f32[4,1,33,180]{3,2,1,0:T(8,128)S(1)}) fusion(f32[4,1,32,180]{3,2,1,0:T(8,128)S(1)} %copy-done.3, f32[4,4,32,180]{3,2,1,0:T(8,128)S(1)} %copy-done, f32[4,5,3,180]{3,2,1,0:T(4,128)S(1)} %copy-done.9), kind=kLoop, calls=%fused_computation.55 | loop fusion | flops 71280 | bytes 622800 | tf_op jit(solution)/shard_map/jit(_where)/broadcast_in_dim | solution.py:52
  31.7 0.7 %copy-done.5 = f32[4,1,33,180]{3,2,1,0:T(8,128)} copy-done((f32[4,1,33,180]{3,2,1,0:T(8,128)}, f32[4,1,33,180]{3,2,1,0:T(8,128)S(1)}, u32[]{:S(2)}) %copy-start.5) | copy-done | bytes 95064
  32.4 0.8 %multiply_bitcast_fusion = (f32[4,33,180]{2,1,0:T(8,128)}, f32[4,33,180]{2,1,0:T(8,128)}, f32[4,33,180]{2,1,0:T(8,128)}) fusion(f32[4,1,33,180]{3,2,1,0:T(8,128)S(1)} %get-tuple-element.5), kind=kLoop, calls=%fused_computation.54 | loop fusion | flops 95040 | bytes 380160 | tf_op jit(solution)/shard_map/mul | solution.py:44
  33.2 0.0 all-to-all-done
  33.2 1.6 %copy.8 = f32[32,4,180]{2,1,0:T(4,128)} copy(f32[32,4,180]{2,0,1:T(8,128)} %bitcast.1) | data formatting | bytes 184320 | tf_op jit(solution)/shard_map/all_to_all | solution.py:156
  34.8 1.7 %all_to_all.17 = f32[32,720]{1,0:T(8,128)} reshape(f32[32,4,180]{2,1,0:T(4,128)} %copy.8) | data formatting | bytes 184320 | tf_op jit(solution)/shard_map/all_to_all | solution.py:156
  36.5 0.9 %slice.175 = f32[32,1]{1,0:T(8,128)S(1)} slice(f32[32,720]{1,0:T(8,128)} %all_to_all.17), slice={[0:32], [719:720]} | slice | bytes 256 | tf_op jit(solution)/shard_map/slice | solution.py:160
  37.4 0.0 copy-done.14
  37.4 3.0 %fusion = f32[32,720]{1,0:T(8,128)S(1)} fusion(f32[720,720]{1,0:T(8,128)} %constant.15.clone, f32[32,720]{1,0:T(8,128)} %all_to_all.17, s32[720]{0:T(1024)S(1)} %copy-done.14, s32[32]{0:T(128)S(1)} %get-tuple-element.3), kind=kOutput, calls=%fused_computation.2 | convolution fusion | flops 199111680 | bytes 2260928 | tf_op jit(solution)/shard_map/dot_general | solution.py:149
  40.4 0.0 copy-start.6
  40.4 0.0 copy-start.10
  40.4 0.0 copy-start.11
  40.4 0.0 copy-start.12
  40.5 0.0 copy-start.13
  40.5 0.0 copy-done.4
  40.5 0.0 copy-done.7
  40.5 1.4 %convolution_select_fusion = f32[32,721]{1,0:T(8,128)S(1)} fusion(f32[32,720]{1,0:T(8,128)S(1)} %fusion, f32[720,721]{1,0:T(8,128)S(1)} %copy-done.4, f32[32,720]{1,0:T(8,128)S(1)} %copy-done.7, f32[32,1]{1,0:T(8,128)S(1)} %slice.175, pred[32]{0:T(512)(128)(4,1)S(1)} %get-tuple-element.2), kind=kOutput, calls=%fused_computation | convolution fusion | flops 199388224 | bytes 2353248 | tf_op jit(solution)/shard_map/dot_general | solution.py:151
  41.8 0.1 slice_bitcast_fusion.6
  42.0 1.6 %collective-permute-start = (f32[1,32,181]{2,1,0:T(8,128)S(1)}, f32[1,32,181]{2,1,0:T(8,128)S(1)}, u32[]{:S(2)}, u32[]{:S(2)}) collective-permute-start(f32[1,32,181]{2,1,0:T(8,128)S(1)} %get-tuple-element.24), channel_id=1, source_target_pairs={{0,1},{1,0},{2,3},{3,2},{4,5},{5,4},{6,7},{7,6},{8,9},{9,8},{10,11... | collective-permute-start | bytes 69512 | tf_op jit(solution)/shard_map/ppermute | solution.py:181
  43.6 0.0 copy-done.11
  43.6 0.0 copy-start.1
  43.6 0.4 fusion.6
  44.1 1.2 %collective-permute-start.1 = (f32[1,32,181]{2,1,0:T(8,128)S(1)}, f32[1,32,181]{2,1,0:T(8,128)S(1)}, u32[]{:S(2)}, u32[]{:S(2)}) collective-permute-start(f32[1,32,181]{2,1,0:T(8,128)S(1)} %get-tuple-element.23), channel_id=1, source_target_pairs={{0,2},{1,3},{2,0},{3,1},{4,6},{5,7},{6,4},{7,5},{8,10},{9,11},{10,... | collective-permute-start | bytes 69512 | tf_op jit(solution)/shard_map/ppermute | solution.py:181
  45.2 1.8 %collective-permute-start.2 = (f32[1,32,181]{2,1,0:T(8,128)S(1)}, f32[1,32,181]{2,1,0:T(8,128)S(1)}, u32[]{:S(2)}, u32[]{:S(2)}) collective-permute-start(f32[1,32,181]{2,1,0:T(8,128)S(1)} %get-tuple-element.22), channel_id=1, source_target_pairs={{0,3},{1,2},{2,1},{3,0},{4,7},{5,6},{6,5},{7,4},{8,11},{9,10},{10,... | collective-permute-start | bytes 69512 | tf_op jit(solution)/shard_map/ppermute | solution.py:181
  47.0 0.0 collective-permute-done
  47.0 2.8 %collective-permute-done.1 = f32[1,32,181]{2,1,0:T(8,128)S(1)} collective-permute-done((f32[1,32,181]{2,1,0:T(8,128)S(1)}, f32[1,32,181]{2,1,0:T(8,128)S(1)}, u32[]{:S(2)}, u32[]{:S(2)}) %collective-permute-start.1) | collective-permute-done | bytes 23200 | tf_op jit(solution)/shard_map/ppermute | solution.py:181
  49.8 1.1 %collective-permute-done.2 = f32[1,32,181]{2,1,0:T(8,128)S(1)} collective-permute-done((f32[1,32,181]{2,1,0:T(8,128)S(1)}, f32[1,32,181]{2,1,0:T(8,128)S(1)}, u32[]{:S(2)}, u32[]{:S(2)}) %collective-permute-start.2) | collective-permute-done | bytes 23200 | tf_op jit(solution)/shard_map/ppermute | solution.py:181
  51.0 0.8 %slice_bitcast_fusion = f32[4,32,180]{2,1,0:T(8,128)} fusion(f32[4,1,32,181]{3,2,0,1:T(8,128)S(1)} %bitcast.36), kind=kLoop, calls=%fused_computation.56 | loop fusion | bytes 184320 | tf_op jit(solution)/shard_map/squeeze | solution.py:203
  51.8 0.0 copy-done.1
  51.8 0.5 fusion.22
  52.3 1.0 %fusion.17 = f32[4,4,32,180]{3,2,1,0:T(8,128)} fusion(f32[4,4,32,180]{3,2,1,0:T(8,128)S(1)} %copy-done, f32[4,4,33,180]{3,2,1,0:T(8,128)S(1)} %fusion.6, f32[4,4,32,181]{3,2,1,0:T(8,128)S(1)} %fusion.22, f32[32]{0:T(128)S(1)} %copy-done.15), kind=kLoop, calls=%fused_computation.30 | loop fusion | flops 460800 | bytes 2211968 | tf_op jit(solution)/shard_map/sub | solution.py:215
  (21 shorter events, 0.2 us)
Async XLA Ops:
  0.6 26.6 %copy-start = (f32[4,4,32,180]{3,2,1,0:T(8,128)S(1)}, f32[4,4,32,180]{3,2,1,0:T(8,128)}, u32[]{:S(2)}) copy-start(f32[4,4,32,180]{3,2,1,0:T(8,128)} %param.6) | copy-start | bytes 1105924
  0.6 18.6 %copy-start.16 = (s32[256]{0:T(256)S(1)}, s32[256]{0:T(256)}, u32[]{:S(2)}) copy-start(s32[256]{0:T(256)} %param.8) | copy-start | bytes 3076
  2.4 27.0 %copy-start.2 = (f32[4,1,32,180]{3,2,1,0:T(8,128)}, f32[4,1,32,180]{3,2,1,0:T(8,128)S(1)}, u32[]{:S(2)}) copy-start(f32[4,1,32,180]{3,2,1,0:T(8,128)S(1)} %get-tuple-element.15) | copy-start | bytes 276484
  3.4 25.8 %collective-permute-start.6 = (f32[4,5,3,180]{3,2,1,0:T(4,128)S(1)}, f32[4,5,3,180]{3,2,1,0:T(4,128)S(1)}, u32[]{:S(2)}, u32[]{:S(2)}) collective-permute-start(f32[4,5,3,180]{3,2,1,0:T(4,128)S(1)} %get-tuple-element.9), channel_id=1, source_target_pairs={{4,0},{8,4},{12,8},{16,12},{20,16},{24,20},{28,24},{5,1},{9,5},{13... | collective-permute-start | bytes 129608 | tf_op jit(solution)/shard_map/ppermute | solution.py:19
  4.7 24.5 %collective-permute-start.5 = (f32[4,5,3,180]{3,2,1,0:T(4,128)S(1)}, f32[4,5,3,180]{3,2,1,0:T(4,128)S(1)}, u32[]{:S(2)}, u32[]{:S(2)}) collective-permute-start(f32[4,5,3,180]{3,2,1,0:T(4,128)S(1)} %get-tuple-element.8), channel_id=1, source_target_pairs={{0,4},{4,8},{8,12},{12,16},{16,20},{20,24},{24,28},{1,5},{5,9},{9,... | collective-permute-start | bytes 129608 | tf_op jit(solution)/shard_map/ppermute | solution.py:17
  8.9 11.7 %collective-permute-start.4 = (f32[4,4,32,3]{3,2,1,0:T(8,128)S(1)}, f32[4,4,32,3]{3,2,1,0:T(8,128)S(1)}, u32[]{:S(2)}, u32[]{:S(2)}) collective-permute-start(f32[4,4,32,3]{3,2,1,0:T(8,128)S(1)} %get-tuple-element.13), channel_id=1, source_target_pairs={{1,0},{2,1},{3,2},{0,3},{5,4},{6,5},{7,6},{4,7},{9,8},{10,9},{11,1... | collective-permute-start | bytes 18440 | tf_op jit(solution)/shard_map/ppermute | solution.py:19
  14.1 13.2 %collective-permute-start.3 = (f32[4,4,32,3]{3,2,1,0:T(8,128)S(1)}, f32[4,4,32,3]{3,2,1,0:T(8,128)S(1)}, u32[]{:S(2)}, u32[]{:S(2)}) collective-permute-start(f32[4,4,32,3]{3,2,1,0:T(8,128)S(1)} %get-tuple-element.12), channel_id=1, source_target_pairs={{0,1},{1,2},{2,3},{3,0},{4,5},{5,6},{6,7},{7,4},{8,9},{9,10},{10,1... | collective-permute-start | bytes 18440 | tf_op jit(solution)/shard_map/ppermute | solution.py:17
  14.1 19.1 %all-to-all-start = ((f32[4,32,180]{2,1,0:T(8,128)}), f32[4,32,180]{2,1,0:T(8,128)}, u32[]{:S(2)}, u32[]{:S(2)}) async-start(f32[4,32,180]{2,1,0:T(8,128)} %get-tuple-element.14), calls=%async_computation | async-start | bytes 262144 | tf_op jit(solution)/shard_map/all_to_all | solution.py:156
  29.2 0.6 %copy-start.8 = (f32[4,5,3,180]{3,2,1,0:T(4,128)}, f32[4,5,3,180]{3,2,1,0:T(4,128)S(1)}, u32[]{:S(2)}) copy-start(f32[4,5,3,180]{3,2,1,0:T(4,128)S(1)} %collective-permute-done.5) | copy-start | bytes 129604
  30.1 0.9 %copy-start.3 = (f32[4,1,32,180]{3,2,1,0:T(8,128)S(1)}, f32[4,1,32,180]{3,2,1,0:T(8,128)}, u32[]{:S(2)}) copy-start(f32[4,1,32,180]{3,2,1,0:T(8,128)} %copy-done.2) | copy-start | bytes 276484
  30.1 0.9 %copy-start.9 = (f32[4,5,3,180]{3,2,1,0:T(4,128)S(1)}, f32[4,5,3,180]{3,2,1,0:T(4,128)}, u32[]{:S(2)}) copy-start(f32[4,5,3,180]{3,2,1,0:T(4,128)} %copy-done.8) | copy-start | bytes 129604
  30.1 7.3 %copy-start.14 = (s32[720]{0:T(1024)S(1)}, s32[720]{0:T(1024)}, u32[]{:S(2)}) copy-start(s32[720]{0:T(1024)} %constant.17.clone) | copy-start | bytes 8644
  31.7 0.7 %copy-start.5 = (f32[4,1,33,180]{3,2,1,0:T(8,128)}, f32[4,1,33,180]{3,2,1,0:T(8,128)S(1)}, u32[]{:S(2)}) copy-start(f32[4,1,33,180]{3,2,1,0:T(8,128)S(1)} %get-tuple-element.5) | copy-start | bytes 285124
  36.5 4.0 %copy-start.4 = (f32[720,721]{1,0:T(8,128)S(1)}, f32[720,721]{1,0:T(8,128)}, u32[]{:S(2)}) copy-start(f32[720,721]{1,0:T(8,128)} %constant.16.clone) | copy-start | bytes 6229444
  36.5 4.0 %copy-start.7 = (f32[32,720]{1,0:T(8,128)S(1)}, f32[32,720]{1,0:T(8,128)}, u32[]{:S(2)}) copy-start(f32[32,720]{1,0:T(8,128)} %all_to_all.17) | copy-start | bytes 276484
  40.4 3.2 %copy-start.6 = (f32[4,1,33,180]{3,2,1,0:T(8,128)S(1)}, f32[4,1,33,180]{3,2,1,0:T(8,128)}, u32[]{:S(2)}) copy-start(f32[4,1,33,180]{3,2,1,0:T(8,128)} %copy-done.5) | copy-start | bytes 285124
  40.4 3.2 %copy-start.10 = (f32[4,33,180]{2,1,0:T(8,128)S(1)}, f32[4,33,180]{2,1,0:T(8,128)}, u32[]{:S(2)}) copy-start(f32[4,33,180]{2,1,0:T(8,128)} %get-tuple-element.16) | copy-start | bytes 285124
  40.4 3.2 %copy-start.11 = (f32[4,33,180]{2,1,0:T(8,128)S(1)}, f32[4,33,180]{2,1,0:T(8,128)}, u32[]{:S(2)}) copy-start(f32[4,33,180]{2,1,0:T(8,128)} %get-tuple-element.17) | copy-start | bytes 285124
  40.4 3.2 %copy-start.12 = (f32[4,33,180]{2,1,0:T(8,128)S(1)}, f32[4,33,180]{2,1,0:T(8,128)}, u32[]{:S(2)}) copy-start(f32[4,33,180]{2,1,0:T(8,128)} %get-tuple-element.18) | copy-start | bytes 285124
  40.5 3.2 %copy-start.13 = (pred[4,33,180]{2,1,0:T(8,128)(4,1)S(1)}, pred[4,33,180]{2,1,0:T(8,128)(4,1)}, u32[]{:S(2)}) copy-start(pred[4,33,180]{2,1,0:T(8,128)(4,1)} %get-tuple-element.4) | copy-start | bytes 71284
  42.0 5.0 %collective-permute-start = (f32[1,32,181]{2,1,0:T(8,128)S(1)}, f32[1,32,181]{2,1,0:T(8,128)S(1)}, u32[]{:S(2)}, u32[]{:S(2)}) collective-permute-start(f32[1,32,181]{2,1,0:T(8,128)S(1)} %get-tuple-element.24), channel_id=1, source_target_pairs={{0,1},{1,0},{2,3},{3,2},{4,5},{5,4},{6,7},{7,6},{8,9},{9,8},{10,11... | collective-permute-start | bytes 69512 | tf_op jit(solution)/shard_map/ppermute | solution.py:181
  43.6 8.2 %copy-start.1 = (f32[4,4,32,182]{3,2,1,0:T(8,128)S(1)}, f32[4,4,32,182]{3,2,1,0:T(8,128)}, u32[]{:S(2)}) copy-start(f32[4,4,32,182]{3,2,1,0:T(8,128)} %get-tuple-element.11) | copy-start | bytes 1118212
  44.1 5.8 %collective-permute-start.1 = (f32[1,32,181]{2,1,0:T(8,128)S(1)}, f32[1,32,181]{2,1,0:T(8,128)S(1)}, u32[]{:S(2)}, u32[]{:S(2)}) collective-permute-start(f32[1,32,181]{2,1,0:T(8,128)S(1)} %get-tuple-element.23), channel_id=1, source_target_pairs={{0,2},{1,3},{2,0},{3,1},{4,6},{5,7},{6,4},{7,5},{8,10},{9,11},{10,... | collective-permute-start | bytes 69512 | tf_op jit(solution)/shard_map/ppermute | solution.py:181
  45.2 5.7 %collective-permute-start.2 = (f32[1,32,181]{2,1,0:T(8,128)S(1)}, f32[1,32,181]{2,1,0:T(8,128)S(1)}, u32[]{:S(2)}, u32[]{:S(2)}) collective-permute-start(f32[1,32,181]{2,1,0:T(8,128)S(1)} %get-tuple-element.22), channel_id=1, source_target_pairs={{0,3},{1,2},{2,1},{3,0},{4,7},{5,6},{6,5},{7,4},{8,11},{9,10},{10,... | collective-permute-start | bytes 69512 | tf_op jit(solution)/shard_map/ppermute | solution.py:181
  51.0 1.3 %copy-start.15 = (f32[32]{0:T(128)S(1)}, f32[32]{0:T(128)}, u32[]{:S(2)}) copy-start(f32[32]{0:T(128)} %fusion.33) | copy-start | bytes 388
